TPU v7x, 512 devices: a whole 4x8x8 slice. The times are simulated.
512 devices in a mesh: col: 16 (over z, x_lo), row: 32 (over y, x_hi, core).
Axes of the slice: x: 4 (x_hi: 2, x_lo: 2; x = x_hi * 2 + x_lo), y: 8, z: 8, core: 2. Of those that a mesh axis runs over, the one named last changes fastest.
Arguments:
- inputs: bfloat16 [1024, 8192], P('row', 'col'), may hold values from -6 to 6
- grad_out: bfloat16 [1024, 8192], P('row', 'col'), may hold values from -6 to 6
- gate_pre: bfloat16 [1024, 16384], P('col', 'row'), may hold values from -8 to 8
- up_pre: bfloat16 [1024, 16384], P('col', 'row'), may hold values from -6 to 6
- gate_weight: bfloat16 [8192, 16384], P('col', 'row'), may hold values from -0.0625 to 0.0625
- up_weight: bfloat16 [8192, 16384], P('col', 'row'), may hold values from -0.0625 to 0.0625
- down_weight: bfloat16 [16384, 8192], P('row', 'col'), may hold values from -0.046875 to 0.046875
Outputs:
- input_grad: bfloat16 [1024, 8192], P('row', 'col')
- gate_grad: bfloat16 [8192, 16384], P('col', 'row')
- up_grad: bfloat16 [8192, 16384], P('col', 'row')
- down_grad: bfloat16 [16384, 8192], P('row', 'col')
All inputs are finite; a program needn't handle non-finite values.
Results may differ from a plain program's by a relative error of at most 0.0049.
Values may be sent and summed in bfloat16 or wider, within the bound.
A program may use at most 64 MiB of HBM per device.

v0:
```python
import math
import jax
import jax.numpy as jnp
from jax import lax
from jax.sharding import PartitionSpec as P


def swiglu_back(hidden_grad, gate_pre, up_pre):
    gate_val = gate_pre.astype(jnp.float32)
    up_val = up_pre.astype(jnp.float32)
    sigmoid_val = jax.nn.sigmoid(gate_val)
    silu_val = gate_val * sigmoid_val
    hidden = (silu_val * up_val).astype(jnp.bfloat16)
    up_term = (hidden_grad * silu_val).astype(jnp.bfloat16)
    gate_term = (
        hidden_grad * up_val * sigmoid_val * (1.0 + gate_val * (1.0 - sigmoid_val))
    ).astype(jnp.bfloat16)
    return (hidden, gate_term, up_term)


def per_device(inputs, grad_out, gate_pre, up_pre, gate_weight, up_weight, down_weight):
    total_tokens = grad_out.shape[0] * lax.axis_size("row")
    grad_scale = 1.0 / math.sqrt(total_tokens)
    grad_all, input_all = (
        lax.all_gather(grad_out, "row", axis=0, tiled=True),
        lax.all_gather(inputs, "row", axis=0, tiled=True),
    )
    partial_hidden = jnp.einsum(
        "td,fd->tf", grad_all, down_weight, preferred_element_type=jnp.float32
    )
    hidden_grad = lax.psum_scatter(partial_hidden, "col", scatter_dimension=0, tiled=True)
    hidden, gate_term, up_term = swiglu_back(hidden_grad, gate_pre, up_pre)
    hidden_all, gate_all, up_all = (
        lax.all_gather(hidden, "col", axis=0, tiled=True),
        lax.all_gather(gate_term, "col", axis=0, tiled=True),
        lax.all_gather(up_term, "col", axis=0, tiled=True),
    )
    down_grad = (
        jnp.einsum("tf,td->fd", hidden_all, grad_all, preferred_element_type=jnp.float32)
        * grad_scale
    ).astype(jnp.bfloat16)
    gate_sum = jnp.einsum("td,tf->df", input_all, gate_all, preferred_element_type=jnp.float32)
    up_sum = jnp.einsum("td,tf->df", input_all, up_all, preferred_element_type=jnp.float32)
    gate_grad = (gate_sum * grad_scale).astype(jnp.bfloat16)
    up_grad = (up_sum * grad_scale).astype(jnp.bfloat16)
    input_grad = lax.psum_scatter(
        jnp.einsum("tf,df->td", gate_all, gate_weight, preferred_element_type=jnp.float32)
        + jnp.einsum("tf,df->td", up_all, up_weight, preferred_element_type=jnp.float32),
        "row",
        scatter_dimension=0,
        tiled=True,
    ).astype(jnp.bfloat16)
    return (input_grad, gate_grad, up_grad, down_grad)


def solution(mesh):
    return jax.shard_map(
        per_device,
        mesh=mesh,
        in_specs=(
            P("row", "col"),
            P("row", "col"),
            P("col", "row"),
            P("col", "row"),
            P("col", "row"),
            P("col", "row"),
            P("row", "col"),
        ),
        out_specs=(P("row", "col"), P("col", "row"), P("col", "row"), P("row", "col")),
        check_vma=False,
    )
```

profile of v0, /device:TPU:16, one launch (start us, length us, event | category | flops | bytes accessed | tf_op | source)
XLA Modules:
  0.0 622.8 jit_solution(12379006136893260064)
XLA Ops:
  7.2 0.7 all-gather.6.cloned.1.call-update
  8.0 90.3 %all-gather.6.cloned.1.call-done = bf16[1024,512]{1,0:T(8,128)(2,1)} async-done(((bf16[32,512]{1,0:T(8,128)(2,1)}), bf16[1024,512]{1,0:T(8,128)(2,1)}) %all-gather.6.cloned.1.call-update) | async-done | bytes 1048592 | tf_op jit(solution)/shard_map/all_gather | solution.py:25
  98.3 3.3 fusion.13
  101.6 0.0 all-gather.8.cloned.1.call-start
  101.7 76.2 %reduce-scatter.3.cloned.1.call-done = f32[64,512]{1,0:T(8,128)} async-done(((f32[1024,512]{1,0:T(8,128)}), f32[64,512]{1,0:T(8,128)}) %reduce-scatter.3.cloned.1.call-update) | async-done | bytes 131088 | tf_op jit(solution)/shard_map/reduce_scatter | solution.py:31
  177.9 1.7 multiply_convert_fusion
  179.6 0.0 all-gather.10.cloned.1.call-start
  179.6 0.5 all-gather.10.cloned.1.call-update
  180.2 0.5 all-gather.12.cloned.1.call-update
  180.8 0.5 all-gather.14.cloned.1.call-update
  181.3 0.0 reduce-scatter.5.cloned.1.call-start
  181.4 69.2 %all-gather.8.cloned.1.call-done = bf16[1024,512]{1,0:T(8,128)(2,1)} async-done(((bf16[64,512]{1,0:T(8,128)(2,1)}), bf16[1024,512]{1,0:T(8,128)(2,1)}) %all-gather.8.cloned.1.call-update) | async-done | bytes 1048592 | tf_op jit(solution)/shard_map/all_gather | solution.py:35
  250.6 2.0 fusion.14
  252.5 72.6 %all-gather.10.cloned.1.call-done = bf16[1024,512]{1,0:T(8,128)(2,1)} async-done(((bf16[64,512]{1,0:T(8,128)(2,1)}), bf16[1024,512]{1,0:T(8,128)(2,1)}) %all-gather.10.cloned.1.call-update) | async-done | bytes 1048592 | tf_op jit(solution)/shard_map/all_gather | solution.py:36
  325.2 3.4 convolution_add_fusion
  328.7 82.4 %all-gather.12.cloned.1.call-done = bf16[1024,512]{1,0:T(8,128)(2,1)} async-done(((bf16[32,512]{1,0:T(8,128)(2,1)}), bf16[1024,512]{1,0:T(8,128)(2,1)}) %all-gather.12.cloned.1.call-update) | async-done | bytes 1048592 | tf_op jit(solution)/shard_map/all_gather | solution.py:26
  411.0 2.0 fusion.4
  413.0 1.0 copy.11
  414.0 2.0 fusion.3
  416.1 1.0 copy.12
  417.1 65.4 %all-gather.14.cloned.1.call-done = bf16[1024,512]{1,0:T(8,128)(2,1)} async-done(((bf16[64,512]{1,0:T(8,128)(2,1)}), bf16[1024,512]{1,0:T(8,128)(2,1)}) %all-gather.14.cloned.1.call-update) | async-done | bytes 1048592 | tf_op jit(solution)/shard_map/all_gather | solution.py:34
  482.4 2.8 fusion.2
  485.2 129.3 %reduce-scatter.5.cloned.1.call-done = f32[32,512]{1,0:T(8,128)} async-done(((f32[1024,512]{1,0:T(8,128)}), f32[32,512]{1,0:T(8,128)}) %reduce-scatter.5.cloned.1.call-update) | async-done | bytes 65552 | tf_op jit(solution)/shard_map/reduce_scatter | solution.py:46
  614.5 1.5 convert_element_type.37
  (21 shorter events, 0.2 us)
Async XLA Ops:
  7.2 91.1 %copy-start = (bf16[512,512]{1,0:T(8,128)(2,1)S(1)}, bf16[512,512]{1,0:T(8,128)(2,1)}, u32[]{:S(2)}) copy-start(bf16[512,512]{1,0:T(8,128)(2,1)} %param.13) | copy-start | bytes 1572868
  7.2 91.1 %all-gather.6.cloned.1.call-start = ((), (), s32[]{:S(2)}) async-start(), calls=%async_computation.2 | async-start | bytes 1081344 | tf_op jit(solution)/shard_map/all_gather | solution.py:25
  7.9 170.0 %copy-start.5 = (bf16[64,512]{1,0:T(8,128)(2,1)S(1)}, bf16[64,512]{1,0:T(8,128)(2,1)}, u32[]{:S(2)}) copy-start(bf16[64,512]{1,0:T(8,128)(2,1)} %param.9) | copy-start | bytes 196612
  7.9 170.0 %copy-start.6 = (bf16[64,512]{1,0:T(8,128)(2,1)S(1)}, bf16[64,512]{1,0:T(8,128)(2,1)}, u32[]{:S(2)}) copy-start(bf16[64,512]{1,0:T(8,128)(2,1)} %param.10) | copy-start | bytes 196612
  7.9 170.0 %reduce-scatter.3.cloned.1.call-start = ((), (), s32[]{:S(2)}) async-start(), calls=%async_computation.3 | async-start | bytes 2228224 | tf_op jit(solution)/shard_map/reduce_scatter | solution.py:31
  101.6 149.0 %copy-start.4 = (bf16[512,512]{1,0:T(8,128)(2,1)S(1)}, bf16[512,512]{1,0:T(8,128)(2,1)}, u32[]{:S(2)}) copy-start(bf16[512,512]{1,0:T(8,128)(2,1)} %param.11) | copy-start | bytes 1572868
  101.6 149.0 %all-gather.8.cloned.1.call-start = ((), (), s32[]{:S(2)}) async-start(), calls=%async_computation.4 | async-start | bytes 1114112 | tf_op jit(solution)/shard_map/all_gather | solution.py:35
  179.6 145.6 %all-gather.10.cloned.1.call-start = ((), (), s32[]{:S(2)}) async-start(), calls=%async_computation.5 | async-start | bytes 1114112 | tf_op jit(solution)/shard_map/all_gather | solution.py:36
  180.2 230.9 %all-gather.12.cloned.1.call-start = ((), (), s32[]{:S(2)}) async-start(), calls=%async_computation.7 | async-start | bytes 1081344 | tf_op jit(solution)/shard_map/all_gather | solution.py:26
  180.8 301.7 %all-gather.14.cloned.1.call-start = ((), (), s32[]{:S(2)}) async-start(), calls=%async_computation.8 | async-start | bytes 1114112 | tf_op jit(solution)/shard_map/all_gather | solution.py:34
  181.3 433.2 %reduce-scatter.5.cloned.1.call-start = ((), (), s32[]{:S(2)}) async-start(), calls=%async_computation.6 | async-start | bytes 2162688 | tf_op jit(solution)/shard_map/reduce_scatter | solution.py:46
  328.6 82.4 %copy-start.2 = (bf16[1024,512]{1,0:T(8,128)(2,1)S(1)}, bf16[1024,512]{1,0:T(8,128)(2,1)}, u32[]{:S(2)}) copy-start(bf16[1024,512]{1,0:T(8,128)(2,1)} %all-gather.8.cloned.1.call-done) | copy-start | bytes 3145732
  328.6 85.4 %copy-start.3 = (bf16[1024,512]{1,0:T(8,128)(2,1)S(1)}, bf16[1024,512]{1,0:T(8,128)(2,1)}, u32[]{:S(2)}) copy-start(bf16[1024,512]{1,0:T(8,128)(2,1)} %all-gather.10.cloned.1.call-done) | copy-start | bytes 3145732
  414.0 68.4 %copy-start.1 = (bf16[1024,512]{1,0:T(8,128)(2,1)S(1)}, bf16[1024,512]{1,0:T(8,128)(2,1)}, u32[]{:S(2)}) copy-start(bf16[1024,512]{1,0:T(8,128)(2,1)} %all-gather.6.cloned.1.call-done) | copy-start | bytes 3145732
Sparse Core Ops, SparseCore 0:
  11.4 86.8 all-gather.5
  101.7 76.1 reduce-scatter.2
  180.6 69.9 all-gather.7
  253.1 72.0 all-gather.9
  328.4 82.5 all-gather.11
  413.0 69.4 all-gather.13
  487.2 127.3 reduce-scatter.4
where the time goes:
time: 623 us
  waiting for transfers between devices  588 us (94%)
  matrix products  15.4 us (2%)
  between operations  14.2 us (2%)
    reduce_scatter x1, waiting for transfers between devices, per_device(): lax.psum_scatter(jnp.einsum('tf,df->td', gate_all, gate_weight, preferred...  129 us
    all_gather x1, waiting for transfers between devices, per_device(): lax.all_gather(grad_out, 'row', axis=0, tiled=True)  90.3 us
    all_gather x1, waiting for transfers between devices, per_device(): lax.all_gather(inputs, 'row', axis=0, tiled=True)  82.4 us
    reduce_scatter x1, waiting for transfers between devices, per_device(): lax.psum_scatter(partial_hidden, 'col', scatter_dimension=0, tiled=True)  76.2 us
    all_gather x1, waiting for transfers between devices, per_device(): lax.all_gather(up_term, 'col', axis=0, tiled=True)  72.6 us
    all_gather x1, waiting for transfers between devices, per_device(): lax.all_gather(gate_term, 'col', axis=0, tiled=True)  69.2 us
    all_gather x1, waiting for transfers between devices, per_device(): lax.all_gather(hidden, 'col', axis=0, tiled=True)  65.4 us
  transfers between devices with their start and end apart: 7, of which 7 were waited for; matrix products, arithmetic and copies ran while one was open for 2% of the time, Pallas kernels for 0%

commit v1 on v0

--- a/solution.py
+++ b/solution.py
@@ -23,7 +23,9 @@
     grad_scale = 1.0 / math.sqrt(total_tokens)
     grad_all, input_all = (
         lax.all_gather(grad_out, "row", axis=0, tiled=True),
-        lax.all_gather(inputs, "row", axis=0, tiled=True),
+        jnp.concatenate(
+            lax.all_to_all(jnp.stack([inputs] * lax.axis_size("row")), "row", 0, 0), axis=0
+        ),
     )
     partial_hidden = jnp.einsum(
         "td,fd->tf", grad_all, down_weight, preferred_element_type=jnp.float32

time: 623 us -> 542 us (0.87)
  waiting for transfers between devices: 588 us -> 469 us
  blocking collectives: 0 us -> 37.5 us
    all_gather x1 -> x0, waiting for transfers between devices: 82.4 us -> none  [per_device(): lax.all_gather(inputs, 'row', axis=0, tiled=True)]
    all_to_all x0 -> x1, blocking collectives: none -> 37.5 us  [per_device(): lax.all_to_all(jnp.stack([inputs] * lax.axis_size('row')), 'row', 0, 0)]
    all_gather x1, waiting for transfers between devices: 65.4 us -> 30.3 us  [per_device(): lax.all_gather(hidden, 'col', axis=0, tiled=True)]
  transfers between devices with their start and end apart: 7 -> 6, of which waited for: 7 -> 6; matrix products, arithmetic and copies ran while one was open for 2% -> 2% of each run, Pallas kernels for 0% -> 0%
where the time goes in v1:
time: 542 us
  waiting for transfers between devices  469 us (87%)
  blocking collectives  37.5 us (7%)
  matrix products  14.2 us (3%)
  between operations  14.2 us (3%)
    reduce_scatter x1, waiting for transfers between devices, per_device(): lax.psum_scatter(jnp.einsum('tf,df->td', gate_all, gate_weight, preferred...  128 us
    all_gather x1, waiting for transfers between devices, per_device(): lax.all_gather(grad_out, 'row', axis=0, tiled=True)  90.3 us
    reduce_scatter x1, waiting for transfers between devices, per_device(): lax.psum_scatter(partial_hidden, 'col', scatter_dimension=0, tiled=True)  76.2 us
    all_gather x1, waiting for transfers between devices, per_device(): lax.all_gather(up_term, 'col', axis=0, tiled=True)  72.6 us
    all_gather x1, waiting for transfers between devices, per_device(): lax.all_gather(gate_term, 'col', axis=0, tiled=True)  69.8 us
    all_to_all x1, blocking collectives, per_device(): lax.all_to_all(jnp.stack([inputs] * lax.axis_size('row')), 'row', 0, 0)  37.5 us
    all_gather x1, waiting for transfers between devices, per_device(): lax.all_gather(hidden, 'col', axis=0, tiled=True)  30.3 us
  transfers between devices with their start and end apart: 6, of which 6 were waited for; matrix products, arithmetic and copies ran while one was open for 2% of the time, Pallas kernels for 0%

profile of v1, /device:TPU:16, one launch (start us, length us, event | category | flops | bytes accessed | tf_op | source)
XLA Modules:
  0.0 541.6 jit_solution(14331241377043208874)
XLA Ops:
  7.2 0.7 all-gather.5.cloned.1.call-update
  8.0 90.3 %all-gather.5.cloned.1.call-done = bf16[1024,512]{1,0:T(8,128)(2,1)} async-done(((bf16[32,512]{1,0:T(8,128)(2,1)}), bf16[1024,512]{1,0:T(8,128)(2,1)}) %all-gather.5.cloned.1.call-update) | async-done | bytes 1048592 | tf_op jit(solution)/shard_map/all_gather | solution.py:25
  98.3 3.3 fusion.13
  101.6 0.0 all-gather.7.cloned.1.call-start
  101.7 76.2 %reduce-scatter.3.cloned.1.call-done = f32[64,512]{1,0:T(8,128)} async-done(((f32[1024,512]{1,0:T(8,128)}), f32[64,512]{1,0:T(8,128)}) %reduce-scatter.3.cloned.1.call-update) | async-done | bytes 131088 | tf_op jit(solution)/shard_map/reduce_scatter | solution.py:33
  177.9 1.7 multiply_convert_fusion
  179.6 0.0 all-gather.9.cloned.1.call-start
  179.7 0.5 all-gather.9.cloned.1.call-update
  180.2 0.5 all-gather.11.cloned.1.call-update
  180.8 69.8 %all-gather.7.cloned.1.call-done = bf16[1024,512]{1,0:T(8,128)(2,1)} async-done(((bf16[64,512]{1,0:T(8,128)(2,1)}), bf16[1024,512]{1,0:T(8,128)(2,1)}) %all-gather.7.cloned.1.call-update) | async-done | bytes 1048592 | tf_op jit(solution)/shard_map/all_gather | solution.py:37
  250.6 2.0 fusion.14
  252.6 72.6 %all-gather.9.cloned.1.call-done = bf16[1024,512]{1,0:T(8,128)(2,1)} async-done(((bf16[64,512]{1,0:T(8,128)(2,1)}), bf16[1024,512]{1,0:T(8,128)(2,1)}) %all-gather.9.cloned.1.call-update) | async-done | bytes 1048592 | tf_op jit(solution)/shard_map/all_gather | solution.py:38
  325.2 3.4 convolution_add_fusion
  328.7 0.7 copy-done.6
  329.4 0.1 stack.2
  329.5 37.5 %all_to_all.5 = bf16[32,32,512]{2,1,0:T(8,128)(2,1)S(1)} all-to-all(bf16[32,32,512]{2,1,0:T(8,128)(2,1)S(1)} %stack.2), channel_id=1, replica_groups=mesh['col'=16,'row'=32] {'row'}, dimensions={0} | all-to-all | bytes 2097152 | tf_op jit(solution)/shard_map/all_to_all | solution.py:27
  367.0 0.7 fusion.4
  367.7 1.0 copy.11
  368.7 2.0 fusion.3
  370.8 1.0 copy.12
  371.8 30.3 %all-gather.11.cloned.1.call-done = bf16[1024,512]{1,0:T(8,128)(2,1)} async-done(((bf16[64,512]{1,0:T(8,128)(2,1)}), bf16[1024,512]{1,0:T(8,128)(2,1)}) %all-gather.11.cloned.1.call-update) | async-done | bytes 1048592 | tf_op jit(solution)/shard_map/all_gather | solution.py:36
  402.1 2.8 fusion.2
  404.8 128.4 %reduce-scatter.5.cloned.1.call-done = f32[32,512]{1,0:T(8,128)} async-done(((f32[1024,512]{1,0:T(8,128)}), f32[32,512]{1,0:T(8,128)}) %reduce-scatter.5.cloned.1.call-update) | async-done | bytes 65552 | tf_op jit(solution)/shard_map/reduce_scatter | solution.py:48
  533.3 1.5 convert_element_type.37
  (20 shorter events, 0.2 us)
Async XLA Ops:
  7.2 91.1 %copy-start = (bf16[512,512]{1,0:T(8,128)(2,1)S(1)}, bf16[512,512]{1,0:T(8,128)(2,1)}, u32[]{:S(2)}) copy-start(bf16[512,512]{1,0:T(8,128)(2,1)} %param.13) | copy-start | bytes 1572868
  7.2 91.1 %all-gather.5.cloned.1.call-start = ((), (), s32[]{:S(2)}) async-start(), calls=%async_computation.3 | async-start | bytes 1081344 | tf_op jit(solution)/shard_map/all_gather | solution.py:25
  7.9 170.0 %copy-start.4 = (bf16[64,512]{1,0:T(8,128)(2,1)S(1)}, bf16[64,512]{1,0:T(8,128)(2,1)}, u32[]{:S(2)}) copy-start(bf16[64,512]{1,0:T(8,128)(2,1)} %param.9) | copy-start | bytes 196612
  7.9 170.0 %copy-start.5 = (bf16[64,512]{1,0:T(8,128)(2,1)S(1)}, bf16[64,512]{1,0:T(8,128)(2,1)}, u32[]{:S(2)}) copy-start(bf16[64,512]{1,0:T(8,128)(2,1)} %param.10) | copy-start | bytes 196612
  7.9 170.0 %reduce-scatter.3.cloned.1.call-start = ((), (), s32[]{:S(2)}) async-start(), calls=%async_computation.4 | async-start | bytes 2228224 | tf_op jit(solution)/shard_map/reduce_scatter | solution.py:33
  101.6 149.0 %copy-start.3 = (bf16[512,512]{1,0:T(8,128)(2,1)S(1)}, bf16[512,512]{1,0:T(8,128)(2,1)}, u32[]{:S(2)}) copy-start(bf16[512,512]{1,0:T(8,128)(2,1)} %param.11) | copy-start | bytes 1572868
  101.6 149.0 %all-gather.7.cloned.1.call-start = ((), (), s32[]{:S(2)}) async-start(), calls=%async_computation.5 | async-start | bytes 1114112 | tf_op jit(solution)/shard_map/all_gather | solution.py:37
  179.6 145.6 %all-gather.9.cloned.1.call-start = ((), (), s32[]{:S(2)}) async-start(), calls=%async_computation.6 | async-start | bytes 1114112 | tf_op jit(solution)/shard_map/all_gather | solution.py:38
  180.2 221.9 %all-gather.11.cloned.1.call-start = ((), (), s32[]{:S(2)}) async-start(), calls=%async_computation.8 | async-start | bytes 1114112 | tf_op jit(solution)/shard_map/all_gather | solution.py:36
  180.8 352.5 %reduce-scatter.5.cloned.1.call-start = ((), (), s32[]{:S(2)}) async-start(), calls=%async_computation.7 | async-start | bytes 2162688 | tf_op jit(solution)/shard_map/reduce_scatter | solution.py:48
  328.6 0.8 copy-start.6
  329.4 37.6 %copy-start.2 = (bf16[1024,512]{1,0:T(8,128)(2,1)S(1)}, bf16[1024,512]{1,0:T(8,128)(2,1)}, u32[]{:S(2)}) copy-start(bf16[1024,512]{1,0:T(8,128)(2,1)} %all-gather.7.cloned.1.call-done) | copy-start | bytes 3145732
  368.7 33.3 %copy-start.1 = (bf16[1024,512]{1,0:T(8,128)(2,1)S(1)}, bf16[1024,512]{1,0:T(8,128)(2,1)}, u32[]{:S(2)}) copy-start(bf16[1024,512]{1,0:T(8,128)(2,1)} %all-gather.5.cloned.1.call-done) | copy-start | bytes 3145732
Sparse Core Ops, SparseCore 0:
  11.4 86.8 all-gather.4
  101.8 76.1 reduce-scatter.2
  180.6 69.9 all-gather.6
  253.1 72.0 all-gather.8
  327.1 74.9 all-gather.10
  406.7 126.5 reduce-scatter.4
